TPU v7x, 32 devices: a whole 2x2x4 slice. The times are simulated.
32 devices in a mesh: node: 8 (over z, y), col: 4 (over x, core).
Axes of the slice: x: 2, y: 2, z: 4, core: 2. Of those that a mesh axis runs over, the one named last changes fastest.
Arguments:
- blocks: float32 [2304, 128, 128], P('node'), may hold values from 0.001 to 1
- owner_row: int32 [8, 288], P('node'), may hold values from 0 to 47, never falling along the last dimension, each value on 1 to 10 neighbouring positions
- block_col: int32 [8, 288], P('node'), may hold values from 0 to 383, as said below
- start: float32 [128, 49152], P('col', 'node'), may hold values from -160 to 160
Outputs:
- basis: float32 [128, 49152], P('col', 'node')
- projected_first: float32 [128, 128], P('col')
- projected: float32 [128, 128], P('col')
Inputs may be any that keep to these rules, and one draw needn't show every extreme that they name: `owner_row`: the stored blocks of one index of node are listed by block row, never falling; every block row has 1 to 10 stored blocks, one has exactly 10. `block_col`: A block stored at index g of node has its block column among the block rows of index g, among the last 24 block rows of index g - 1, or among the first 24 block rows of index g + 1, cyclically over node; every index has blocks at both of those bounds.
All inputs are finite; a program needn't handle non-finite values.
Results may differ from a plain program's by a relative error of at most 0.0003.
Values sent between devices are 32-bit elements; how exact they have to be, the bound alone decides.
No kernel may reach another device: no remote copies, remote signals or barrier semaphores. Data moves between devices by JAX's collectives and lax.ppermute only.
A program may use at most 128 MiB of HBM per device.

v0:
```python
import jax
import jax.numpy as jnp
from jax import lax
from jax.sharding import PartitionSpec as P

DEGREE = 4
ITERS = 2
precise = lax.Precision.HIGHEST
center = 1.025
half_width = 0.975


def extended_2(cells, sides, width):
    for axis, dim in sides:
        count = lax.axis_size(axis)
        head = lax.slice_in_dim(cells, 0, width, axis=dim)
        tail = lax.slice_in_dim(cells, cells.shape[dim] - width, cells.shape[dim], axis=dim)
        cells = jnp.concatenate(
            [
                lax.ppermute(tail, axis, [(i, (i + 1) % count) for i in range(count)]),
                cells,
                lax.ppermute(head, axis, [((i + 1) % count, i) for i in range(count)]),
            ],
            axis=dim,
        )
    return cells


def chebyshev(panel, operate):
    previous = panel
    current = (operate(panel) - center * panel) / half_width
    for step in range(DEGREE - 1):
        following = 2.0 * (operate(current) - center * current) / half_width - previous
        previous = current
        current = following
    return current


def body(blocks, owner_row, block_col, start):
    cols_here = start.shape[0]
    width = start.shape[1]
    block = blocks.shape[1]
    rows_blocks = width // block
    groups = lax.axis_size("node")
    nodes = width * groups
    row_ids = owner_row[0]
    col_ids = block_col[0]
    onehot = (row_ids[None, :] == jnp.arange(rows_blocks, dtype=jnp.int32)[:, None]).astype(
        jnp.float32
    )
    degree = jnp.einsum("rn,ni->ri", onehot, jnp.sum(blocks, axis=2), precision=precise).reshape(
        width
    )
    node_me = lax.axis_index("node")
    owner = col_ids // rows_blocks
    side = (owner - node_me + 1) % groups
    lookup = (side - 1) * rows_blocks + col_ids % rows_blocks + rows_blocks
    col_me = lax.axis_index("col")

    def operate(panel):
        extended = extended_2(panel, (("node", 1),), rows_blocks * block)
        pieces = extended.reshape(cols_here, -1, block)
        gathered = jnp.take(pieces, lookup, axis=1)
        product = jnp.einsum("nij,knj->nki", blocks, gathered, precision=precise)
        summed = jnp.einsum("rn,nki->kri", onehot, product, precision=precise).reshape(
            cols_here, width
        )
        return panel - summed / degree[None, :]

    def to_rows(panel):
        return lax.all_to_all(panel, "col", split_axis=1, concat_axis=0, tiled=True)

    basis = start
    results = []
    for step in range(ITERS):
        filtered = chebyshev(basis, operate)
        rows_now = to_rows(filtered)
        gram_part = jnp.dot(rows_now, rows_now.T, precision=precise) / nodes
        gram = lax.psum(gram_part, ("node", "col"))
        factor = jnp.linalg.cholesky(gram)
        rows_basis = jax.scipy.linalg.solve_triangular(factor, rows_now, lower=True)
        basis = lax.all_to_all(rows_basis, "col", split_axis=0, concat_axis=1, tiled=True)
        image = to_rows(operate(basis))
        part = jnp.dot(rows_basis, image.T, precision=precise) / nodes
        totals = lax.psum((part,), ("node", "col"))
        results.append(
            tuple(
                (
                    lax.dynamic_slice_in_dim(total, col_me * cols_here, cols_here, 0)
                    for total in totals
                )
            )[0]
        )
    return (basis, results[0], results[-1])


def solution(mesh):
    placed = (P("node", None, None), P("node", None), P("node", None), P("col", "node"))
    return jax.shard_map(
        body,
        mesh=mesh,
        in_specs=placed,
        out_specs=(P("col", "node"), P("col", None), P("col", None)),
        check_vma=False,
    )
```

profile of v0, /device:TPU:0, one launch (start us, length us, event | category | flops | bytes accessed | tf_op | source)
XLA Modules:
  0.0 1225.8 jit_solution(599584303518014007)
XLA Ops:
  14.1 9.6 reduce_sum.9
  23.9 20.3 %collective-permute-done = f32[32,6144]{1,0:T(8,128)S(1)} collective-permute-done((f32[32,6144]{1,0:T(8,128)}, f32[32,6144]{1,0:T(8,128)S(1)}, u32[]{:S(2)}, u32[]{:S(2)}) %collective-permute-start) | collective-permute-done | bytes 786464 | tf_op jit(solution)/shard_map/ppermute | solution.py:20
  48.1 3.3 gather_fusion
  51.4 33.1 %fusion.16 = f32[288,32,128]{2,1,0:T(8,128)S(1)} fusion(f32[288,128,128]{2,1,0:T(8,128)} %param.9, f32[288,32,128]{2,1,0:T(8,128)} %gather_fusion, pred[288]{0:T(512)(128)(4,1)S(1)} %get-tuple-element.25), kind=kOutput, calls=%fused_computation.25 | convolution fusion | flops 1813118976 | bytes 28311840 | tf_op jit(solution)/shard_map/nij,knj->nki/dot_general | solution.py:64
  84.5 4.8 fusion.34
  90.8 3.7 collective-permute-start.3
  94.4 29.1 %collective-permute-done.2 = f32[32,6144]{1,0:T(8,128)S(1)} collective-permute-done((f32[32,6144]{1,0:T(8,128)S(1)}, f32[32,6144]{1,0:T(8,128)S(1)}, u32[]{:S(2)}, u32[]{:S(2)}) %collective-permute-start.2) | collective-permute-done | bytes 786464 | tf_op jit(solution)/shard_map/ppermute | solution.py:20
  123.6 3.1 collective-permute-done.3
  127.0 3.3 gather_fusion.1
  130.3 33.2 %fusion.14 = f32[288,32,128]{2,1,0:T(8,128)S(1)} fusion(f32[288,128,128]{2,1,0:T(8,128)} %param.9, f32[288,32,128]{2,1,0:T(8,128)} %gather_fusion.1, pred[288]{0:T(512)(128)(4,1)S(1)} %get-tuple-element.25), kind=kOutput, calls=%fused_computation.23 | convolution fusion | flops 1813118976 | bytes 28311840 | tf_op jit(solution)/shard_map/nij,knj->nki/dot_general | solution.py:64
  163.5 4.8 fusion.32
  169.1 4.7 collective-permute-start.5
  173.8 28.7 %collective-permute-done.4 = f32[32,6144]{1,0:T(8,128)S(1)} collective-permute-done((f32[32,6144]{1,0:T(8,128)S(1)}, f32[32,6144]{1,0:T(8,128)S(1)}, u32[]{:S(2)}, u32[]{:S(2)}) %collective-permute-start.4) | collective-permute-done | bytes 786464 | tf_op jit(solution)/shard_map/ppermute | solution.py:20
  202.5 3.8 collective-permute-done.5
  206.6 3.6 gather_fusion.2
  210.2 33.4 %fusion.12 = f32[288,32,128]{2,1,0:T(8,128)S(1)} fusion(f32[288,128,128]{2,1,0:T(8,128)} %param.9, f32[288,32,128]{2,1,0:T(8,128)} %gather_fusion.2, pred[288]{0:T(512)(128)(4,1)S(1)} %get-tuple-element.25), kind=kOutput, calls=%fused_computation.21 | convolution fusion | flops 1813118976 | bytes 28311840 | tf_op jit(solution)/shard_map/nij,knj->nki/dot_general | solution.py:64
  243.6 4.8 fusion.30
  249.2 4.7 collective-permute-start.7
  253.9 28.5 %collective-permute-done.6 = f32[32,6144]{1,0:T(8,128)S(1)} collective-permute-done((f32[32,6144]{1,0:T(8,128)S(1)}, f32[32,6144]{1,0:T(8,128)S(1)}, u32[]{:S(2)}, u32[]{:S(2)}) %collective-permute-start.6) | collective-permute-done | bytes 786464 | tf_op jit(solution)/shard_map/ppermute | solution.py:20
  282.4 4.0 collective-permute-done.7
  286.7 3.5 gather_fusion.3
  290.2 33.2 %fusion.10 = f32[288,32,128]{2,1,0:T(8,128)S(1)} fusion(f32[288,128,128]{2,1,0:T(8,128)} %param.9, f32[288,32,128]{2,1,0:T(8,128)} %gather_fusion.3, pred[288]{0:T(512)(128)(4,1)S(1)} %get-tuple-element.25), kind=kOutput, calls=%fused_computation.19 | convolution fusion | flops 1813118976 | bytes 28311840 | tf_op jit(solution)/shard_map/nij,knj->nki/dot_general | solution.py:64
  323.4 4.8 fusion.28
  328.6 14.2 %all_to_all.105 = f32[32,4,1536]{2,0,1:T(8,128)S(1)} all-to-all(f32[32,4,1536]{2,0,1:T(8,128)S(1)} %bitcast.287), channel_id=1, replica_groups=mesh['node'=8,'col'=4] {'col'}, dimensions={1} | all-to-all | bytes 1572864 | tf_op jit(solution)/shard_map/all_to_all | solution.py:71
  344.6 114.6 %all-reduce.5.cloned.1.call-done = f32[128,128]{0,1:T(8,128)} async-done(((f32[128,128]{0,1:T(8,128)}), f32[128,128]{0,1:T(8,128)}) %all-reduce.5.cloned.1.call-update) | async-done | bytes 65552 | tf_op jit(solution)/shard_map/psum | solution.py:79
  461.0 11.7 cholesky.44
  474.1 9.8 custom-call.6
  484.7 15.4 %all_to_all.106 = f32[4,32,1536]{2,1,0:T(8,128)S(1)} all-to-all(f32[4,32,1536]{2,1,0:T(8,128)S(1)} %bitcast.280), channel_id=1, replica_groups=mesh['node'=8,'col'=4] {'col'}, dimensions={0} | all-to-all | bytes 1572864 | tf_op jit(solution)/shard_map/all_to_all | solution.py:82
  501.0 4.4 collective-permute-start.9
  506.5 27.8 %collective-permute-done.8 = f32[32,6144]{1,0:T(8,128)} collective-permute-done((f32[32,6144]{1,0:T(8,128)S(1)}, f32[32,6144]{1,0:T(8,128)}, u32[]{:S(2)}, u32[]{:S(2)}) %collective-permute-start.8) | collective-permute-done | bytes 786464 | tf_op jit(solution)/shard_map/ppermute | solution.py:20
  537.8 3.3 gather_fusion.4
  541.1 33.1 %fusion.8 = f32[288,32,128]{2,1,0:T(8,128)S(1)} fusion(f32[288,128,128]{2,1,0:T(8,128)} %param.9, f32[288,32,128]{2,1,0:T(8,128)} %gather_fusion.4, pred[288]{0:T(512)(128)(4,1)S(1)} %get-tuple-element.25), kind=kOutput, calls=%fused_computation.17 | convolution fusion | flops 1813118976 | bytes 28311840 | tf_op jit(solution)/shard_map/nij,knj->nki/dot_general | solution.py:64
  574.2 4.8 fusion.26
  580.1 4.0 collective-permute-start.11
  584.1 28.3 %collective-permute-done.10 = f32[32,6144]{1,0:T(8,128)S(1)} collective-permute-done((f32[32,6144]{1,0:T(8,128)S(1)}, f32[32,6144]{1,0:T(8,128)S(1)}, u32[]{:S(2)}, u32[]{:S(2)}) %collective-permute-start.10) | collective-permute-done | bytes 786464 | tf_op jit(solution)/shard_map/ppermute | solution.py:20
  612.4 3.7 collective-permute-done.11
  616.5 3.5 gather_fusion.5
  620.0 33.2 %fusion.6 = f32[288,32,128]{2,1,0:T(8,128)S(1)} fusion(f32[288,128,128]{2,1,0:T(8,128)} %param.9, f32[288,32,128]{2,1,0:T(8,128)} %gather_fusion.5, pred[288]{0:T(512)(128)(4,1)S(1)} %get-tuple-element.25), kind=kOutput, calls=%fused_computation.15 | convolution fusion | flops 1813118976 | bytes 28311840 | tf_op jit(solution)/shard_map/nij,knj->nki/dot_general | solution.py:64
  653.2 4.8 fusion.24
  658.8 4.7 collective-permute-start.13
  663.5 28.5 %collective-permute-done.12 = f32[32,6144]{1,0:T(8,128)S(1)} collective-permute-done((f32[32,6144]{1,0:T(8,128)S(1)}, f32[32,6144]{1,0:T(8,128)S(1)}, u32[]{:S(2)}, u32[]{:S(2)}) %collective-permute-start.12) | collective-permute-done | bytes 786464 | tf_op jit(solution)/shard_map/ppermute | solution.py:20
  695.1 3.6 gather_fusion.6
  698.7 33.5 %fusion.4 = f32[288,32,128]{2,1,0:T(8,128)S(1)} fusion(f32[288,128,128]{2,1,0:T(8,128)} %param.9, f32[288,32,128]{2,1,0:T(8,128)} %gather_fusion.6, pred[288]{0:T(512)(128)(4,1)S(1)} %get-tuple-element.25), kind=kOutput, calls=%fused_computation.13 | convolution fusion | flops 1813118976 | bytes 28311840 | tf_op jit(solution)/shard_map/nij,knj->nki/dot_general | solution.py:64
  732.2 4.8 fusion.22
  738.1 4.7 collective-permute-start.15
  745.4 25.3 %collective-permute-done.14 = f32[32,6144]{1,0:T(8,128)} collective-permute-done((f32[32,6144]{1,0:T(8,128)S(1)}, f32[32,6144]{1,0:T(8,128)}, u32[]{:S(2)}, u32[]{:S(2)}) %collective-permute-start.14) | collective-permute-done | bytes 786464 | tf_op jit(solution)/shard_map/ppermute | solution.py:20
  770.7 3.5 collective-permute-done.15
  776.1 3.5 gather_fusion.7
  779.6 33.2 %fusion.2 = f32[288,32,128]{2,1,0:T(8,128)S(1)} fusion(f32[288,128,128]{2,1,0:T(8,128)} %param.9, f32[288,32,128]{2,1,0:T(8,128)} %gather_fusion.7, pred[288]{0:T(512)(128)(4,1)S(1)} %get-tuple-element.25), kind=kOutput, calls=%fused_computation.11 | convolution fusion | flops 1813118976 | bytes 28311840 | tf_op jit(solution)/shard_map/nij,knj->nki/dot_general | solution.py:64
  812.8 4.8 fusion.63
  818.7 3.5 fusion.106
  822.3 14.7 %all_to_all.107 = f32[32,4,1536]{2,0,1:T(8,128)S(1)} all-to-all(f32[32,4,1536]{2,0,1:T(8,128)S(1)} %get-tuple-element.28), channel_id=1, replica_groups=mesh['node'=8,'col'=4] {'col'}, dimensions={1} | all-to-all | bytes 1572864 | tf_op jit(solution)/shard_map/all_to_all | solution.py:71
  838.4 115.4 %all-reduce.7.cloned.1.call-done = f32[128,128]{0,1:T(8,128)} async-done(((f32[128,128]{0,1:T(8,128)}), f32[128,128]{0,1:T(8,128)}) %all-reduce.7.cloned.1.call-update) | async-done | bytes 65552 | tf_op jit(solution)/shard_map/psum | solution.py:79
  955.6 11.7 cholesky.55
  968.7 9.8 custom-call.7
  979.3 15.4 %all_to_all.108 = f32[4,32,1536]{2,1,0:T(8,128)S(1)} all-to-all(f32[4,32,1536]{2,1,0:T(8,128)S(1)} %bitcast.281), channel_id=1, replica_groups=mesh['node'=8,'col'=4] {'col'}, dimensions={0} | all-to-all | bytes 1572864 | tf_op jit(solution)/shard_map/all_to_all | solution.py:82
  998.6 4.7 all-to-all-start.4
  1004.3 27.4 %collective-permute-done.17 = f32[32,6144]{1,0:T(8,128)} collective-permute-done((f32[32,6144]{1,0:T(8,128)}, f32[32,6144]{1,0:T(8,128)}, u32[]{:S(2)}, u32[]{:S(2)}) %collective-permute-start.17) | collective-permute-done | bytes 786464 | tf_op jit(solution)/shard_map/ppermute | solution.py:22
  1034.4 3.3 gather_fusion.8
  1037.7 33.1 %fusion = f32[288,32,128]{2,1,0:T(8,128)S(1)} fusion(f32[288,128,128]{2,1,0:T(8,128)} %param.9, f32[288,32,128]{2,1,0:T(8,128)} %gather_fusion.8, pred[288]{0:T(512)(128)(4,1)S(1)} %get-tuple-element.25), kind=kOutput, calls=%fused_computation.9 | convolution fusion | flops 1813118976 | bytes 28311840 | tf_op jit(solution)/shard_map/nij,knj->nki/dot_general | solution.py:64
  1070.9 4.8 fusion.66
  1079.2 3.5 all-to-all-start.5
  1085.3 9.0 all-to-all-done.5
  1095.7 121.1 %all-reduce.9.cloned.1.call-done = (f32[128,128]{0,1:T(8,128)}, f32[128,128]{0,1:T(8,128)}) async-done(((f32[128,128]{0,1:T(8,128)}, f32[128,128]{0,1:T(8,128)}), (f32[128,128]{0,1:T(8,128)}, f32[128,128]{0,1:T(8,128)})) %all-reduce.9.cloned.1.call-update) | async-done | bytes 131088 | tf_op jit(solution)/shard_map/psum | solution.py:85
  (133 shorter events, 61.5 us)
Async XLA Ops:
  7.2 452.0 %all-reduce.5.cloned.1.call-start = ((), (), s32[]{:S(2)}) async-start(), calls=%async_computation.6 | async-start | bytes 131072 | tf_op jit(solution)/shard_map/psum | solution.py:79
  7.2 37.0 %collective-permute-start = (f32[32,6144]{1,0:T(8,128)}, f32[32,6144]{1,0:T(8,128)S(1)}, u32[]{:S(2)}, u32[]{:S(2)}) collective-permute-start(f32[32,6144]{1,0:T(8,128)} %param.12), channel_id=1, source_target_pairs={{0,4},{4,8},{8,12},{12,16},{16,20},{20,24},{24,28},{28,0},{1,5},{5... | collective-permute-start | bytes 2359304 | tf_op jit(solution)/shard_map/ppermute | solution.py:20
  10.2 36.2 %collective-permute-start.1 = (f32[32,6144]{1,0:T(8,128)}, f32[32,6144]{1,0:T(8,128)}, u32[]{:S(2)}, u32[]{:S(2)}) collective-permute-start(f32[32,6144]{1,0:T(8,128)} %param.12), channel_id=1, source_target_pairs={{4,0},{8,4},{12,8},{16,12},{20,16},{24,20},{28,24},{0,28},{5,1},{9... | collective-permute-start | bytes 2359304 | tf_op jit(solution)/shard_map/ppermute | solution.py:22
  14.0 9.6 copy-start.24
  14.0 32.4 %copy-start = (f32[32,6144]{1,0:T(8,128)S(1)}, f32[32,6144]{1,0:T(8,128)}, u32[]{:S(2)}) copy-start(f32[32,6144]{1,0:T(8,128)} %param.12) | copy-start | bytes 2359300
  44.2 0.9 copy-start.23
  89.3 34.3 %copy-start.7 = (f32[32,128,48]{1,2,0:T(8,128)}, f32[32,128,48]{1,2,0:T(8,128)S(1)}, u32[]{:S(2)}) copy-start(f32[32,128,48]{1,2,0:T(8,128)S(1)} %fusion.34) | copy-start | bytes 2359300
  89.7 33.9 %collective-permute-start.2 = (f32[32,6144]{1,0:T(8,128)S(1)}, f32[32,6144]{1,0:T(8,128)S(1)}, u32[]{:S(2)}, u32[]{:S(2)}) collective-permute-start(f32[32,6144]{1,0:T(8,128)S(1)} %broadcast_multiply_fusion.1), channel_id=1, source_target_pairs={{0,4},{4,8},{8,12},{12,16},{16,20},{20,24},{24,28},{28,0},{1,5},{5... | collective-permute-start | bytes 2359304 | tf_op jit(solution)/shard_map/ppermute | solution.py:20
  90.8 35.9 %collective-permute-start.3 = (f32[32,6144]{1,0:T(8,128)S(1)}, f32[32,6144]{1,0:T(8,128)S(1)}, u32[]{:S(2)}, u32[]{:S(2)}) collective-permute-start(f32[32,6144]{1,0:T(8,128)S(1)} %broadcast_multiply_fusion.1), channel_id=1, source_target_pairs={{4,0},{8,4},{12,8},{16,12},{20,16},{24,20},{28,24},{0,28},{5,1},{9... | collective-permute-start | bytes 2359304 | tf_op jit(solution)/shard_map/ppermute | solution.py:22
  163.5 4.8 copy-start.8
  169.0 37.3 %copy-start.10 = (f32[32,6144]{1,0:T(8,128)}, f32[32,6144]{1,0:T(8,128)S(1)}, u32[]{:S(2)}) copy-start(f32[32,6144]{1,0:T(8,128)S(1)} %fusion.90) | copy-start | bytes 2359300
  169.0 33.5 %collective-permute-start.4 = (f32[32,6144]{1,0:T(8,128)S(1)}, f32[32,6144]{1,0:T(8,128)S(1)}, u32[]{:S(2)}, u32[]{:S(2)}) collective-permute-start(f32[32,6144]{1,0:T(8,128)S(1)} %fusion.90), channel_id=1, source_target_pairs={{0,4},{4,8},{8,12},{12,16},{16,20},{20,24},{24,28},{28,0},{1,5},{5... | collective-permute-start | bytes 2359304 | tf_op jit(solution)/shard_map/ppermute | solution.py:20
  169.1 37.2 %collective-permute-start.5 = (f32[32,6144]{1,0:T(8,128)S(1)}, f32[32,6144]{1,0:T(8,128)S(1)}, u32[]{:S(2)}, u32[]{:S(2)}) collective-permute-start(f32[32,6144]{1,0:T(8,128)S(1)} %fusion.90), channel_id=1, source_target_pairs={{4,0},{8,4},{12,8},{16,12},{20,16},{24,20},{28,24},{0,28},{5,1},{9... | collective-permute-start | bytes 2359304 | tf_op jit(solution)/shard_map/ppermute | solution.py:22
  243.6 4.8 copy-start.9
  243.6 4.8 copy-start.11
  249.1 37.3 %copy-start.19 = (f32[32,6144]{1,0:T(8,128)}, f32[32,6144]{1,0:T(8,128)S(1)}, u32[]{:S(2)}) copy-start(f32[32,6144]{1,0:T(8,128)S(1)} %fusion.86) | copy-start | bytes 2359300
  249.1 33.3 %collective-permute-start.6 = (f32[32,6144]{1,0:T(8,128)S(1)}, f32[32,6144]{1,0:T(8,128)S(1)}, u32[]{:S(2)}, u32[]{:S(2)}) collective-permute-start(f32[32,6144]{1,0:T(8,128)S(1)} %fusion.86), channel_id=1, source_target_pairs={{0,4},{4,8},{8,12},{12,16},{16,20},{20,24},{24,28},{28,0},{1,5},{5... | collective-permute-start | bytes 2359304 | tf_op jit(solution)/shard_map/ppermute | solution.py:20
  249.2 37.2 %collective-permute-start.7 = (f32[32,6144]{1,0:T(8,128)S(1)}, f32[32,6144]{1,0:T(8,128)S(1)}, u32[]{:S(2)}, u32[]{:S(2)}) collective-permute-start(f32[32,6144]{1,0:T(8,128)S(1)} %fusion.86), channel_id=1, source_target_pairs={{4,0},{8,4},{12,8},{16,12},{20,16},{24,20},{28,24},{0,28},{5,1},{9... | collective-permute-start | bytes 2359304 | tf_op jit(solution)/shard_map/ppermute | solution.py:22
  323.4 4.8 copy-start.12
  323.4 4.8 copy-start.20
  344.3 609.5 %all-reduce.7.cloned.1.call-start = ((), (), s32[]{:S(2)}) async-start(), calls=%async_computation.7 | async-start | bytes 131072 | tf_op jit(solution)/shard_map/psum | solution.py:79
  484.7 15.5 %copy-start.15 = (f32[128,1536]{1,0:T(8,128)}, f32[128,1536]{1,0:T(8,128)S(1)}, u32[]{:S(2)}) copy-start(f32[128,1536]{1,0:T(8,128)S(1)} %fusion.123) | copy-start | bytes 2359300
  500.1 5.3 copy-start.1
  500.2 37.3 %copy-start.3 = (f32[4,4,8,1536]{3,2,0,1:T(8,128)}, f32[4,4,8,1536]{3,2,0,1:T(8,128)S(1)}, u32[]{:S(2)}) copy-start(f32[4,4,8,1536]{3,2,0,1:T(8,128)S(1)} %copy.168) | copy-start | bytes 2359300
  500.2 34.1 %collective-permute-start.8 = (f32[32,6144]{1,0:T(8,128)S(1)}, f32[32,6144]{1,0:T(8,128)}, u32[]{:S(2)}, u32[]{:S(2)}) collective-permute-start(f32[32,6144]{1,0:T(8,128)S(1)} %bitcast.269), channel_id=1, source_target_pairs={{0,4},{4,8},{8,12},{12,16},{16,20},{20,24},{24,28},{28,0},{1,5},{5... | collective-permute-start | bytes 2359304 | tf_op jit(solution)/shard_map/ppermute | solution.py:20
  501.0 36.4 %collective-permute-start.9 = (f32[32,6144]{1,0:T(8,128)S(1)}, f32[32,6144]{1,0:T(8,128)S(1)}, u32[]{:S(2)}, u32[]{:S(2)}) collective-permute-start(f32[32,6144]{1,0:T(8,128)S(1)} %bitcast.270), channel_id=1, source_target_pairs={{4,0},{8,4},{12,8},{16,12},{20,16},{24,20},{28,24},{0,28},{5,1},{9... | collective-permute-start | bytes 2359304 | tf_op jit(solution)/shard_map/ppermute | solution.py:22
  574.2 4.8 copy-start.4
  579.3 33.1 %collective-permute-start.10 = (f32[32,6144]{1,0:T(8,128)S(1)}, f32[32,6144]{1,0:T(8,128)S(1)}, u32[]{:S(2)}, u32[]{:S(2)}) collective-permute-start(f32[32,6144]{1,0:T(8,128)S(1)} %broadcast_multiply_fusion), channel_id=1, source_target_pairs={{0,4},{4,8},{8,12},{12,16},{16,20},{20,24},{24,28},{28,0},{1,5},{5... | collective-permute-start | bytes 2359304 | tf_op jit(solution)/shard_map/ppermute | solution.py:20
  580.1 36.1 %collective-permute-start.11 = (f32[32,6144]{1,0:T(8,128)S(1)}, f32[32,6144]{1,0:T(8,128)S(1)}, u32[]{:S(2)}, u32[]{:S(2)}) collective-permute-start(f32[32,6144]{1,0:T(8,128)S(1)} %broadcast_multiply_fusion), channel_id=1, source_target_pairs={{4,0},{8,4},{12,8},{16,12},{20,16},{24,20},{28,24},{0,28},{5,1},{9... | collective-permute-start | bytes 2359304 | tf_op jit(solution)/shard_map/ppermute | solution.py:22
  653.2 4.8 copy-start.5
  658.0 34.0 %copy-start.13 = (f32[32,128,48]{1,2,0:T(8,128)}, f32[32,128,48]{1,2,0:T(8,128)S(1)}, u32[]{:S(2)}) copy-start(f32[32,128,48]{1,2,0:T(8,128)S(1)} %fusion.24) | copy-start | bytes 2359300
  658.7 33.2 %collective-permute-start.12 = (f32[32,6144]{1,0:T(8,128)S(1)}, f32[32,6144]{1,0:T(8,128)S(1)}, u32[]{:S(2)}, u32[]{:S(2)}) collective-permute-start(f32[32,6144]{1,0:T(8,128)S(1)} %fusion.76), channel_id=1, source_target_pairs={{0,4},{4,8},{8,12},{12,16},{16,20},{20,24},{24,28},{28,0},{1,5},{5... | collective-permute-start | bytes 2359304 | tf_op jit(solution)/shard_map/ppermute | solution.py:20
  658.8 36.0 %collective-permute-start.13 = (f32[32,6144]{1,0:T(8,128)S(1)}, f32[32,6144]{1,0:T(8,128)S(1)}, u32[]{:S(2)}, u32[]{:S(2)}) collective-permute-start(f32[32,6144]{1,0:T(8,128)S(1)} %fusion.76), channel_id=1, source_target_pairs={{4,0},{8,4},{12,8},{16,12},{20,16},{24,20},{28,24},{0,28},{5,1},{9... | collective-permute-start | bytes 2359304 | tf_op jit(solution)/shard_map/ppermute | solution.py:22
  732.2 4.8 copy-start.6
  732.2 4.8 copy-start.14
  738.1 32.6 %copy-start.21 = (f32[32,6144]{1,0:T(8,128)}, f32[32,6144]{1,0:T(8,128)S(1)}, u32[]{:S(2)}) copy-start(f32[32,6144]{1,0:T(8,128)S(1)} %fusion.72) | copy-start | bytes 2359300
  738.1 32.6 %collective-permute-start.14 = (f32[32,6144]{1,0:T(8,128)S(1)}, f32[32,6144]{1,0:T(8,128)}, u32[]{:S(2)}, u32[]{:S(2)}) collective-permute-start(f32[32,6144]{1,0:T(8,128)S(1)} %fusion.72), channel_id=1, source_target_pairs={{0,4},{4,8},{8,12},{12,16},{16,20},{20,24},{24,28},{28,0},{1,5},{5... | collective-permute-start | bytes 2359304 | tf_op jit(solution)/shard_map/ppermute | solution.py:20
  738.1 36.1 %collective-permute-start.15 = (f32[32,6144]{1,0:T(8,128)S(1)}, f32[32,6144]{1,0:T(8,128)}, u32[]{:S(2)}, u32[]{:S(2)}) collective-permute-start(f32[32,6144]{1,0:T(8,128)S(1)} %fusion.72), channel_id=1, source_target_pairs={{4,0},{8,4},{12,8},{16,12},{20,16},{24,20},{28,24},{0,28},{5,1},{9... | collective-permute-start | bytes 2359304 | tf_op jit(solution)/shard_map/ppermute | solution.py:22
  812.8 6.0 copy-start.2
  812.8 5.9 copy-start.22
  979.3 25.0 %copy-start.17 = (f32[128,1536]{1,0:T(8,128)}, f32[128,1536]{1,0:T(8,128)S(1)}, u32[]{:S(2)}) copy-start(f32[128,1536]{1,0:T(8,128)S(1)} %fusion.120) | copy-start | bytes 2359300
  995.7 36.1 %collective-permute-start.17 = (f32[32,6144]{1,0:T(8,128)}, f32[32,6144]{1,0:T(8,128)}, u32[]{:S(2)}, u32[]{:S(2)}) collective-permute-start(f32[32,6144]{1,0:T(8,128)} %bitcast.69), channel_id=1, source_target_pairs={{4,0},{8,4},{12,8},{16,12},{20,16},{24,20},{28,24},{0,28},{5,1},{9... | collective-permute-start | bytes 2359304 | tf_op jit(solution)/shard_map/ppermute | solution.py:22
  998.6 34.4 %collective-permute-start.16 = (f32[32,6144]{1,0:T(8,128)}, f32[32,6144]{1,0:T(8,128)}, u32[]{:S(2)}, u32[]{:S(2)}) collective-permute-start(f32[32,6144]{1,0:T(8,128)} %bitcast.69), channel_id=1, source_target_pairs={{0,4},{4,8},{8,12},{12,16},{16,20},{20,24},{24,28},{28,0},{1,5},{5... | collective-permute-start | bytes 2359304 | tf_op jit(solution)/shard_map/ppermute | solution.py:20
  998.6 80.6 %all-to-all-start.4 = ((f32[32,4,1536]{2,0,1:T(8,128)}), f32[32,4,1536]{2,0,1:T(8,128)}, u32[]{:S(2)}, u32[]{:S(2)}) async-start(f32[32,4,1536]{2,0,1:T(8,128)} %get-tuple-element.27), calls=%async_computation.4 | async-start | bytes 1572864 | tf_op jit(solution)/shard_map/all_to_all | solution.py:71
  1070.8 11.9 copy-start.16
  1075.6 18.6 %copy-start.18 = (f32[128,1536]{1,0:T(8,128)S(1)}, f32[128,1536]{1,0:T(8,128)}, u32[]{:S(2)}) copy-start(f32[128,1536]{1,0:T(8,128)} %copy-done.17) | copy-start | bytes 2359300
  1079.2 15.1 %all-to-all-start.5 = ((f32[32,4,1536]{2,0,1:T(8,128)}), f32[32,4,1536]{2,0,1:T(8,128)S(1)}, u32[]{:S(2)}, u32[]{:S(2)}) async-start(f32[32,4,1536]{2,0,1:T(8,128)} %fusion.93), calls=%async_computation.5 | async-start | bytes 1572864 | tf_op jit(solution)/shard_map/all_to_all | solution.py:71
  1082.7 134.1 %all-reduce.9.cloned.1.call-start = ((), (), s32[]{:S(2)}) async-start(), calls=%async_computation.8 | async-start | bytes 262144 | tf_op jit(solution)/shard_map/psum | solution.py:85
Sparse Core Ops, SparseCore 0:
  344.4 114.7 all-reduce.4
  838.6 115.2 all-reduce.6
  1095.8 120.9 all-reduce.8
where the time goes:
time: 1230 us
  waiting for transfers between devices  628 us (51%)
  matrix products  350 us (28%)
  other arithmetic  73.4 us (6%)
  blocking collectives  59.7 us (5%)
  starting transfers between devices  51.4 us (4%)
  local copies, waits for them, and re-layouts  47.9 us (4%)
  between operations  14.7 us (1%)
    dot_general x9, matrix products, operate(): product = jnp.einsum('nij,knj->nki', blocks, gathered, precision=precise)  299 us
    psum x2, waiting for transfers between devices, body(): gram = lax.psum(gram_part, ('node', 'col'))  230 us
    ppermute x9, waiting for transfers between devices, extended_2(): lax.ppermute(tail, axis, [(i, (i + 1) % count) for i in range(count)])  216 us
    psum x1, waiting for transfers between devices, body(): totals = lax.psum((part,), ('node', 'col'))  121 us
    ppermute x9, waiting for transfers between devices, extended_2(): lax.ppermute(head, axis, [((i + 1) % count, i) for i in range(count)])  51.6 us
    dot_general x9, matrix products, operate(): jnp.einsum('rn,nki->kri', onehot, product, precision=precise)  42.9 us
    ppermute x9, starting transfers between devices, extended_2(): lax.ppermute(head, axis, [((i + 1) % count, i) for i in range(count)])  36.9 us
    gather x9, local copies, waits for them, and re-layouts, operate(): gathered = jnp.take(pieces, lookup, axis=1)  30.9 us
  transfers between devices with their start and end apart: 23, of which 21 were waited for; matrix products, arithmetic and copies ran while one was open for 5% of the time, Pallas kernels for 0%

commit v1 on v0

--- a/solution.py
+++ b/solution.py
@@ -76,7 +76,8 @@
         filtered = chebyshev(basis, operate)
         rows_now = to_rows(filtered)
         gram_part = jnp.dot(rows_now, rows_now.T, precision=precise) / nodes
-        gram = lax.psum(gram_part, ("node", "col"))
+        parts = lax.all_gather(gram_part, ("node", "col"))
+        gram = jnp.sum(parts, axis=0)
         factor = jnp.linalg.cholesky(gram)
         rows_basis = jax.scipy.linalg.solve_triangular(factor, rows_now, lower=True)
         basis = lax.all_to_all(rows_basis, "col", split_axis=0, concat_axis=1, tiled=True)

time: 1230 us -> 1110 us (0.902)
  waiting for transfers between devices: 628 us -> 505 us
    psum x2 -> x0, waiting for transfers between devices: 230 us -> none  [body(): gram = lax.psum(gram_part, ('node', 'col'))]
    all_gather x0 -> x2, waiting for transfers between devices: none -> 107 us  [body(): parts = lax.all_gather(gram_part, ('node', 'col'))]
  transfers between devices with their start and end apart: 23 -> 23, of which waited for: 21 -> 21; matrix products, arithmetic and copies ran while one was open for 5% -> 6% of each run, Pallas kernels for 0% -> 0%
where the time goes in v1:
time: 1110 us; the launch traced here: 1100 us
  waiting for transfers between devices  505 us (45%)
  matrix products  350 us (32%)
  other arithmetic  75.2 us (7%)
  blocking collectives  56.9 us (5%)
  starting transfers between devices  51.5 us (5%)
  local copies, waits for them, and re-layouts  45.3 us (4%)
  between operations  14.7 us (1%)
    dot_general x9, matrix products, operate(): product = jnp.einsum('nij,knj->nki', blocks, gathered, precision=precise)  299 us
    ppermute x9, waiting for transfers between devices, extended_2(): lax.ppermute(tail, axis, [(i, (i + 1) % count) for i in range(count)])  217 us
    psum x1, waiting for transfers between devices, body(): totals = lax.psum((part,), ('node', 'col'))  121 us
    all_gather x2, waiting for transfers between devices, body(): parts = lax.all_gather(gram_part, ('node', 'col'))  107 us
    ppermute x9, waiting for transfers between devices, extended_2(): lax.ppermute(head, axis, [((i + 1) % count, i) for i in range(count)])  51.3 us
    dot_general x9, matrix products, operate(): jnp.einsum('rn,nki->kri', onehot, product, precision=precise)  42.9 us
    ppermute x9, starting transfers between devices, extended_2(): lax.ppermute(head, axis, [((i + 1) % count, i) for i in range(count)])  35.7 us
    gather x9, local copies, waits for them, and re-layouts, operate(): gathered = jnp.take(pieces, lookup, axis=1)  30.9 us
  transfers between devices with their start and end apart: 23, of which 21 were waited for; matrix products, arithmetic and copies ran while one was open for 6% of the time, Pallas kernels for 0%

profile of v1, /device:TPU:0, one launch (start us, length us, event | category | flops | bytes accessed | tf_op | source)
XLA Modules:
  0.0 1099.2 jit_solution(10104638384728532389)
XLA Ops:
  14.1 9.6 reduce_sum.27
  23.9 20.3 %collective-permute-done = f32[32,6144]{1,0:T(8,128)S(1)} collective-permute-done((f32[32,6144]{1,0:T(8,128)}, f32[32,6144]{1,0:T(8,128)S(1)}, u32[]{:S(2)}, u32[]{:S(2)}) %collective-permute-start) | collective-permute-done | bytes 786464 | tf_op jit(solution)/shard_map/ppermute | solution.py:20
  48.1 3.3 gather_fusion
  51.4 33.1 %fusion.16 = f32[288,32,128]{2,1,0:T(8,128)S(1)} fusion(f32[288,128,128]{2,1,0:T(8,128)} %param.9, f32[288,32,128]{2,1,0:T(8,128)} %gather_fusion, pred[288]{0:T(512)(128)(4,1)S(1)} %get-tuple-element.10), kind=kOutput, calls=%fused_computation.25 | convolution fusion | flops 1813118976 | bytes 28311840 | tf_op jit(solution)/shard_map/nij,knj->nki/dot_general | solution.py:64
  84.5 4.8 fusion.34
  90.8 3.7 collective-permute-start.3
  94.4 29.1 %collective-permute-done.2 = f32[32,6144]{1,0:T(8,128)S(1)} collective-permute-done((f32[32,6144]{1,0:T(8,128)S(1)}, f32[32,6144]{1,0:T(8,128)S(1)}, u32[]{:S(2)}, u32[]{:S(2)}) %collective-permute-start.2) | collective-permute-done | bytes 786464 | tf_op jit(solution)/shard_map/ppermute | solution.py:20
  123.6 3.1 collective-permute-done.3
  127.0 3.3 gather_fusion.1
  130.3 33.2 %fusion.14 = f32[288,32,128]{2,1,0:T(8,128)S(1)} fusion(f32[288,128,128]{2,1,0:T(8,128)} %param.9, f32[288,32,128]{2,1,0:T(8,128)} %gather_fusion.1, pred[288]{0:T(512)(128)(4,1)S(1)} %get-tuple-element.10), kind=kOutput, calls=%fused_computation.23 | convolution fusion | flops 1813118976 | bytes 28311840 | tf_op jit(solution)/shard_map/nij,knj->nki/dot_general | solution.py:64
  163.5 4.8 fusion.32
  169.1 4.7 collective-permute-start.5
  173.8 28.7 %collective-permute-done.4 = f32[32,6144]{1,0:T(8,128)S(1)} collective-permute-done((f32[32,6144]{1,0:T(8,128)S(1)}, f32[32,6144]{1,0:T(8,128)S(1)}, u32[]{:S(2)}, u32[]{:S(2)}) %collective-permute-start.4) | collective-permute-done | bytes 786464 | tf_op jit(solution)/shard_map/ppermute | solution.py:20
  202.5 3.8 collective-permute-done.5
  206.6 3.6 gather_fusion.2
  210.2 33.4 %fusion.12 = f32[288,32,128]{2,1,0:T(8,128)S(1)} fusion(f32[288,128,128]{2,1,0:T(8,128)} %param.9, f32[288,32,128]{2,1,0:T(8,128)} %gather_fusion.2, pred[288]{0:T(512)(128)(4,1)S(1)} %get-tuple-element.10), kind=kOutput, calls=%fused_computation.21 | convolution fusion | flops 1813118976 | bytes 28311840 | tf_op jit(solution)/shard_map/nij,knj->nki/dot_general | solution.py:64
  243.6 4.8 fusion.30
  249.2 4.7 collective-permute-start.7
  253.9 28.5 %collective-permute-done.6 = f32[32,6144]{1,0:T(8,128)S(1)} collective-permute-done((f32[32,6144]{1,0:T(8,128)S(1)}, f32[32,6144]{1,0:T(8,128)S(1)}, u32[]{:S(2)}, u32[]{:S(2)}) %collective-permute-start.6) | collective-permute-done | bytes 786464 | tf_op jit(solution)/shard_map/ppermute | solution.py:20
  282.4 4.0 collective-permute-done.7
  286.7 3.5 gather_fusion.3
  290.2 33.2 %fusion.10 = f32[288,32,128]{2,1,0:T(8,128)S(1)} fusion(f32[288,128,128]{2,1,0:T(8,128)} %param.9, f32[288,32,128]{2,1,0:T(8,128)} %gather_fusion.3, pred[288]{0:T(512)(128)(4,1)S(1)} %get-tuple-element.10), kind=kOutput, calls=%fused_computation.19 | convolution fusion | flops 1813118976 | bytes 28311840 | tf_op jit(solution)/shard_map/nij,knj->nki/dot_general | solution.py:64
  323.4 4.8 fusion.28
  328.6 14.2 %all_to_all.105 = f32[32,4,1536]{2,0,1:T(8,128)S(1)} all-to-all(f32[32,4,1536]{2,0,1:T(8,128)S(1)} %bitcast.289), channel_id=1, replica_groups=mesh['node'=8,'col'=4] {'col'}, dimensions={1} | all-to-all | bytes 1572864 | tf_op jit(solution)/shard_map/all_to_all | solution.py:71
  344.6 53.5 %all-gather.5.cloned.1.call-done = f32[4096,128]{1,0:T(8,128)} async-done(((f32[128,128]{1,0:T(8,128)}), f32[4096,128]{1,0:T(8,128)}) %all-gather.5.cloned.1.call-update) | async-done | bytes 2097168 | tf_op jit(solution)/shard_map/all_gather | solution.py:79
  399.9 11.7 %cholesky.44 = f32[128,128]{1,0:T(8,128)S(1)} custom-call(f32[128,128]{1,0:T(8,128)S(1)} %fusion.125), custom_call_target="Cholesky" | custom-call | tf_op jit(solution)/shard_map/jit(cholesky)/cholesky | solution.py:81
  413.0 9.8 custom-call.6
  423.6 14.2 %all_to_all.106 = f32[4,32,1536]{2,1,0:T(8,128)S(1)} all-to-all(f32[4,32,1536]{2,1,0:T(8,128)S(1)} %bitcast.282), channel_id=1, replica_groups=mesh['node'=8,'col'=4] {'col'}, dimensions={0} | all-to-all | bytes 1572864 | tf_op jit(solution)/shard_map/all_to_all | solution.py:83
  439.3 3.8 collective-permute-start.9
  444.2 28.4 %collective-permute-done.8 = f32[32,6144]{1,0:T(8,128)} collective-permute-done((f32[32,6144]{1,0:T(8,128)S(1)}, f32[32,6144]{1,0:T(8,128)}, u32[]{:S(2)}, u32[]{:S(2)}) %collective-permute-start.8) | collective-permute-done | bytes 786464 | tf_op jit(solution)/shard_map/ppermute | solution.py:20
  475.6 3.3 gather_fusion.4
  478.9 33.1 %fusion.8 = f32[288,32,128]{2,1,0:T(8,128)S(1)} fusion(f32[288,128,128]{2,1,0:T(8,128)} %param.9, f32[288,32,128]{2,1,0:T(8,128)} %gather_fusion.4, pred[288]{0:T(512)(128)(4,1)S(1)} %get-tuple-element.10), kind=kOutput, calls=%fused_computation.17 | convolution fusion | flops 1813118976 | bytes 28311840 | tf_op jit(solution)/shard_map/nij,knj->nki/dot_general | solution.py:64
  512.0 4.8 fusion.26
  518.4 3.5 collective-permute-start.11
  521.9 28.8 %collective-permute-done.10 = f32[32,6144]{1,0:T(8,128)S(1)} collective-permute-done((f32[32,6144]{1,0:T(8,128)S(1)}, f32[32,6144]{1,0:T(8,128)S(1)}, u32[]{:S(2)}, u32[]{:S(2)}) %collective-permute-start.10) | collective-permute-done | bytes 786464 | tf_op jit(solution)/shard_map/ppermute | solution.py:20
  553.3 3.5 gather_fusion.5
  556.8 33.2 %fusion.6 = f32[288,32,128]{2,1,0:T(8,128)S(1)} fusion(f32[288,128,128]{2,1,0:T(8,128)} %param.9, f32[288,32,128]{2,1,0:T(8,128)} %gather_fusion.5, pred[288]{0:T(512)(128)(4,1)S(1)} %get-tuple-element.10), kind=kOutput, calls=%fused_computation.15 | convolution fusion | flops 1813118976 | bytes 28311840 | tf_op jit(solution)/shard_map/nij,knj->nki/dot_general | solution.py:64
  590.0 4.8 fusion.24
  595.8 4.4 collective-permute-start.13
  600.3 27.3 %collective-permute-done.12 = f32[32,6144]{1,0:T(8,128)S(1)} collective-permute-done((f32[32,6144]{1,0:T(8,128)S(1)}, f32[32,6144]{1,0:T(8,128)S(1)}, u32[]{:S(2)}, u32[]{:S(2)}) %collective-permute-start.12) | collective-permute-done | bytes 786464 | tf_op jit(solution)/shard_map/ppermute | solution.py:20
  627.6 3.8 collective-permute-done.13
  631.7 3.6 gather_fusion.6
  635.3 33.5 %fusion.4 = f32[288,32,128]{2,1,0:T(8,128)S(1)} fusion(f32[288,128,128]{2,1,0:T(8,128)} %param.9, f32[288,32,128]{2,1,0:T(8,128)} %gather_fusion.6, pred[288]{0:T(512)(128)(4,1)S(1)} %get-tuple-element.10), kind=kOutput, calls=%fused_computation.13 | convolution fusion | flops 1813118976 | bytes 28311840 | tf_op jit(solution)/shard_map/nij,knj->nki/dot_general | solution.py:64
  668.8 4.8 fusion.22
  674.7 4.7 collective-permute-start.15
  682.0 25.7 %collective-permute-done.14 = f32[32,6144]{1,0:T(8,128)} collective-permute-done((f32[32,6144]{1,0:T(8,128)S(1)}, f32[32,6144]{1,0:T(8,128)}, u32[]{:S(2)}, u32[]{:S(2)}) %collective-permute-start.14) | collective-permute-done | bytes 786464 | tf_op jit(solution)/shard_map/ppermute | solution.py:20
  707.6 4.4 collective-permute-done.15
  714.0 3.5 gather_fusion.7
  717.4 33.2 %fusion.2 = f32[288,32,128]{2,1,0:T(8,128)S(1)} fusion(f32[288,128,128]{2,1,0:T(8,128)} %param.9, f32[288,32,128]{2,1,0:T(8,128)} %gather_fusion.7, pred[288]{0:T(512)(128)(4,1)S(1)} %get-tuple-element.10), kind=kOutput, calls=%fused_computation.11 | convolution fusion | flops 1813118976 | bytes 28311840 | tf_op jit(solution)/shard_map/nij,knj->nki/dot_general | solution.py:64
  750.6 4.8 fusion.63
  756.5 3.5 fusion.106
  760.1 14.3 %all_to_all.107 = f32[32,4,1536]{2,0,1:T(8,128)S(1)} all-to-all(f32[32,4,1536]{2,0,1:T(8,128)S(1)} %get-tuple-element.13), channel_id=1, replica_groups=mesh['node'=8,'col'=4] {'col'}, dimensions={1} | all-to-all | bytes 1572864 | tf_op jit(solution)/shard_map/all_to_all | solution.py:71
  775.9 53.6 %all-gather.7.cloned.1.call-done = f32[4096,128]{1,0:T(8,128)} async-done(((f32[128,128]{1,0:T(8,128)}), f32[4096,128]{1,0:T(8,128)}) %all-gather.7.cloned.1.call-update) | async-done | bytes 2097168 | tf_op jit(solution)/shard_map/all_gather | solution.py:79
  831.2 11.7 %cholesky.55 = f32[128,128]{1,0:T(8,128)S(1)} custom-call(f32[128,128]{1,0:T(8,128)S(1)} %fusion.122), custom_call_target="Cholesky" | custom-call | tf_op jit(solution)/shard_map/jit(cholesky)/cholesky | solution.py:81
  844.3 9.8 custom-call.7
  855.0 14.2 %all_to_all.108 = f32[4,32,1536]{2,1,0:T(8,128)S(1)} all-to-all(f32[4,32,1536]{2,1,0:T(8,128)S(1)} %bitcast.283), channel_id=1, replica_groups=mesh['node'=8,'col'=4] {'col'}, dimensions={0} | all-to-all | bytes 1572864 | tf_op jit(solution)/shard_map/all_to_all | solution.py:83
  873.1 4.7 all-to-all-start.4
  878.8 27.3 %collective-permute-done.17 = f32[32,6144]{1,0:T(8,128)} collective-permute-done((f32[32,6144]{1,0:T(8,128)}, f32[32,6144]{1,0:T(8,128)}, u32[]{:S(2)}, u32[]{:S(2)}) %collective-permute-start.17) | collective-permute-done | bytes 786464 | tf_op jit(solution)/shard_map/ppermute | solution.py:22
  908.8 3.3 gather_fusion.8
  912.1 33.1 %fusion = f32[288,32,128]{2,1,0:T(8,128)S(1)} fusion(f32[288,128,128]{2,1,0:T(8,128)} %param.9, f32[288,32,128]{2,1,0:T(8,128)} %gather_fusion.8, pred[288]{0:T(512)(128)(4,1)S(1)} %get-tuple-element.10), kind=kOutput, calls=%fused_computation.9 | convolution fusion | flops 1813118976 | bytes 28311840 | tf_op jit(solution)/shard_map/nij,knj->nki/dot_general | solution.py:64
  945.3 4.8 fusion.66
  953.6 3.5 all-to-all-start.5
  959.7 9.0 all-to-all-done.5
  970.1 120.9 %all-reduce.3.cloned.1.call-done = (f32[128,128]{1,0:T(8,128)}, f32[128,128]{1,0:T(8,128)}) async-done(((f32[128,128]{1,0:T(8,128)}, f32[128,128]{1,0:T(8,128)}), (f32[128,128]{1,0:T(8,128)}, f32[128,128]{1,0:T(8,128)})) %all-reduce.3.cloned.1.call-update) | async-done | bytes 131088 | tf_op jit(solution)/shard_map/psum | solution.py:86
  (133 shorter events, 60.9 us)
Async XLA Ops:
  7.2 390.9 %all-gather.5.cloned.1.call-start = ((), (), s32[]{:S(2)}) async-start(), calls=%async_computation.6 | async-start | bytes 2162688 | tf_op jit(solution)/shard_map/all_gather | solution.py:79
  7.2 37.0 %collective-permute-start = (f32[32,6144]{1,0:T(8,128)}, f32[32,6144]{1,0:T(8,128)S(1)}, u32[]{:S(2)}, u32[]{:S(2)}) collective-permute-start(f32[32,6144]{1,0:T(8,128)} %param.12), channel_id=1, source_target_pairs={{0,4},{4,8},{8,12},{12,16},{16,20},{20,24},{24,28},{28,0},{1,5},{5... | collective-permute-start | bytes 2359304 | tf_op jit(solution)/shard_map/ppermute | solution.py:20
  10.2 36.2 %collective-permute-start.1 = (f32[32,6144]{1,0:T(8,128)}, f32[32,6144]{1,0:T(8,128)}, u32[]{:S(2)}, u32[]{:S(2)}) collective-permute-start(f32[32,6144]{1,0:T(8,128)} %param.12), channel_id=1, source_target_pairs={{4,0},{8,4},{12,8},{16,12},{20,16},{24,20},{28,24},{0,28},{5,1},{9... | collective-permute-start | bytes 2359304 | tf_op jit(solution)/shard_map/ppermute | solution.py:22
  14.0 9.6 copy-start.24
  14.0 32.4 %copy-start = (f32[32,6144]{1,0:T(8,128)S(1)}, f32[32,6144]{1,0:T(8,128)}, u32[]{:S(2)}) copy-start(f32[32,6144]{1,0:T(8,128)} %param.12) | copy-start | bytes 2359300
  44.2 0.9 copy-start.23
  89.3 34.3 %copy-start.7 = (f32[32,128,48]{1,2,0:T(8,128)}, f32[32,128,48]{1,2,0:T(8,128)S(1)}, u32[]{:S(2)}) copy-start(f32[32,128,48]{1,2,0:T(8,128)S(1)} %fusion.34) | copy-start | bytes 2359300
  89.7 33.9 %collective-permute-start.2 = (f32[32,6144]{1,0:T(8,128)S(1)}, f32[32,6144]{1,0:T(8,128)S(1)}, u32[]{:S(2)}, u32[]{:S(2)}) collective-permute-start(f32[32,6144]{1,0:T(8,128)S(1)} %broadcast_multiply_fusion.1), channel_id=1, source_target_pairs={{0,4},{4,8},{8,12},{12,16},{16,20},{20,24},{24,28},{28,0},{1,5},{5... | collective-permute-start | bytes 2359304 | tf_op jit(solution)/shard_map/ppermute | solution.py:20
  90.8 35.9 %collective-permute-start.3 = (f32[32,6144]{1,0:T(8,128)S(1)}, f32[32,6144]{1,0:T(8,128)S(1)}, u32[]{:S(2)}, u32[]{:S(2)}) collective-permute-start(f32[32,6144]{1,0:T(8,128)S(1)} %broadcast_multiply_fusion.1), channel_id=1, source_target_pairs={{4,0},{8,4},{12,8},{16,12},{20,16},{24,20},{28,24},{0,28},{5,1},{9... | collective-permute-start | bytes 2359304 | tf_op jit(solution)/shard_map/ppermute | solution.py:22
  163.5 4.8 copy-start.8
  169.0 37.3 %copy-start.10 = (f32[32,6144]{1,0:T(8,128)}, f32[32,6144]{1,0:T(8,128)S(1)}, u32[]{:S(2)}) copy-start(f32[32,6144]{1,0:T(8,128)S(1)} %fusion.90) | copy-start | bytes 2359300
  169.0 33.5 %collective-permute-start.4 = (f32[32,6144]{1,0:T(8,128)S(1)}, f32[32,6144]{1,0:T(8,128)S(1)}, u32[]{:S(2)}, u32[]{:S(2)}) collective-permute-start(f32[32,6144]{1,0:T(8,128)S(1)} %fusion.90), channel_id=1, source_target_pairs={{0,4},{4,8},{8,12},{12,16},{16,20},{20,24},{24,28},{28,0},{1,5},{5... | collective-permute-start | bytes 2359304 | tf_op jit(solution)/shard_map/ppermute | solution.py:20
  169.1 37.2 %collective-permute-start.5 = (f32[32,6144]{1,0:T(8,128)S(1)}, f32[32,6144]{1,0:T(8,128)S(1)}, u32[]{:S(2)}, u32[]{:S(2)}) collective-permute-start(f32[32,6144]{1,0:T(8,128)S(1)} %fusion.90), channel_id=1, source_target_pairs={{4,0},{8,4},{12,8},{16,12},{20,16},{24,20},{28,24},{0,28},{5,1},{9... | collective-permute-start | bytes 2359304 | tf_op jit(solution)/shard_map/ppermute | solution.py:22
  243.6 4.8 copy-start.9
  243.6 4.8 copy-start.11
  249.1 37.3 %copy-start.19 = (f32[32,6144]{1,0:T(8,128)}, f32[32,6144]{1,0:T(8,128)S(1)}, u32[]{:S(2)}) copy-start(f32[32,6144]{1,0:T(8,128)S(1)} %fusion.86) | copy-start | bytes 2359300
  249.1 33.3 %collective-permute-start.6 = (f32[32,6144]{1,0:T(8,128)S(1)}, f32[32,6144]{1,0:T(8,128)S(1)}, u32[]{:S(2)}, u32[]{:S(2)}) collective-permute-start(f32[32,6144]{1,0:T(8,128)S(1)} %fusion.86), channel_id=1, source_target_pairs={{0,4},{4,8},{8,12},{12,16},{16,20},{20,24},{24,28},{28,0},{1,5},{5... | collective-permute-start | bytes 2359304 | tf_op jit(solution)/shard_map/ppermute | solution.py:20
  249.2 37.2 %collective-permute-start.7 = (f32[32,6144]{1,0:T(8,128)S(1)}, f32[32,6144]{1,0:T(8,128)S(1)}, u32[]{:S(2)}, u32[]{:S(2)}) collective-permute-start(f32[32,6144]{1,0:T(8,128)S(1)} %fusion.86), channel_id=1, source_target_pairs={{4,0},{8,4},{12,8},{16,12},{20,16},{24,20},{28,24},{0,28},{5,1},{9... | collective-permute-start | bytes 2359304 | tf_op jit(solution)/shard_map/ppermute | solution.py:22
  323.4 4.8 copy-start.12
  323.4 4.8 copy-start.20
  344.3 485.1 %all-gather.7.cloned.1.call-start = ((), (), s32[]{:S(2)}) async-start(), calls=%async_computation.7 | async-start | bytes 2162688 | tf_op jit(solution)/shard_map/all_gather | solution.py:79
  423.6 14.2 %copy-start.15 = (f32[128,1536]{1,0:T(8,128)}, f32[128,1536]{1,0:T(8,128)S(1)}, u32[]{:S(2)}) copy-start(f32[128,1536]{1,0:T(8,128)S(1)} %fusion.123) | copy-start | bytes 2359300
  437.8 5.3 copy-start.1
  437.9 37.4 %copy-start.3 = (f32[4,4,8,1536]{3,2,0,1:T(8,128)}, f32[4,4,8,1536]{3,2,0,1:T(8,128)S(1)}, u32[]{:S(2)}) copy-start(f32[4,4,8,1536]{3,2,0,1:T(8,128)S(1)} %copy.134) | copy-start | bytes 2359300
  437.9 34.7 %collective-permute-start.8 = (f32[32,6144]{1,0:T(8,128)S(1)}, f32[32,6144]{1,0:T(8,128)}, u32[]{:S(2)}, u32[]{:S(2)}) collective-permute-start(f32[32,6144]{1,0:T(8,128)S(1)} %bitcast.271), channel_id=1, source_target_pairs={{0,4},{4,8},{8,12},{12,16},{16,20},{20,24},{24,28},{28,0},{1,5},{5... | collective-permute-start | bytes 2359304 | tf_op jit(solution)/shard_map/ppermute | solution.py:20
  439.3 35.9 %collective-permute-start.9 = (f32[32,6144]{1,0:T(8,128)S(1)}, f32[32,6144]{1,0:T(8,128)S(1)}, u32[]{:S(2)}, u32[]{:S(2)}) collective-permute-start(f32[32,6144]{1,0:T(8,128)S(1)} %bitcast.272), channel_id=1, source_target_pairs={{4,0},{8,4},{12,8},{16,12},{20,16},{24,20},{28,24},{0,28},{5,1},{9... | collective-permute-start | bytes 2359304 | tf_op jit(solution)/shard_map/ppermute | solution.py:22
  512.0 4.8 copy-start.4
  517.1 33.6 %collective-permute-start.10 = (f32[32,6144]{1,0:T(8,128)S(1)}, f32[32,6144]{1,0:T(8,128)S(1)}, u32[]{:S(2)}, u32[]{:S(2)}) collective-permute-start(f32[32,6144]{1,0:T(8,128)S(1)} %broadcast_multiply_fusion), channel_id=1, source_target_pairs={{0,4},{4,8},{8,12},{12,16},{16,20},{20,24},{24,28},{28,0},{1,5},{5... | collective-permute-start | bytes 2359304 | tf_op jit(solution)/shard_map/ppermute | solution.py:20
  518.4 34.6 %collective-permute-start.11 = (f32[32,6144]{1,0:T(8,128)S(1)}, f32[32,6144]{1,0:T(8,128)S(1)}, u32[]{:S(2)}, u32[]{:S(2)}) collective-permute-start(f32[32,6144]{1,0:T(8,128)S(1)} %broadcast_multiply_fusion), channel_id=1, source_target_pairs={{4,0},{8,4},{12,8},{16,12},{20,16},{24,20},{28,24},{0,28},{5,1},{9... | collective-permute-start | bytes 2359304 | tf_op jit(solution)/shard_map/ppermute | solution.py:22
  590.0 4.8 copy-start.5
  594.8 32.8 %copy-start.13 = (f32[32,128,48]{1,2,0:T(8,128)}, f32[32,128,48]{1,2,0:T(8,128)S(1)}, u32[]{:S(2)}) copy-start(f32[32,128,48]{1,2,0:T(8,128)S(1)} %fusion.24) | copy-start | bytes 2359300
  595.5 32.1 %collective-permute-start.12 = (f32[32,6144]{1,0:T(8,128)S(1)}, f32[32,6144]{1,0:T(8,128)S(1)}, u32[]{:S(2)}, u32[]{:S(2)}) collective-permute-start(f32[32,6144]{1,0:T(8,128)S(1)} %fusion.76), channel_id=1, source_target_pairs={{0,4},{4,8},{8,12},{12,16},{16,20},{20,24},{24,28},{28,0},{1,5},{5... | collective-permute-start | bytes 2359304 | tf_op jit(solution)/shard_map/ppermute | solution.py:20
  595.8 35.5 %collective-permute-start.13 = (f32[32,6144]{1,0:T(8,128)S(1)}, f32[32,6144]{1,0:T(8,128)S(1)}, u32[]{:S(2)}, u32[]{:S(2)}) collective-permute-start(f32[32,6144]{1,0:T(8,128)S(1)} %fusion.76), channel_id=1, source_target_pairs={{4,0},{8,4},{12,8},{16,12},{20,16},{24,20},{28,24},{0,28},{5,1},{9... | collective-permute-start | bytes 2359304 | tf_op jit(solution)/shard_map/ppermute | solution.py:22
  668.8 4.8 copy-start.6
  668.8 4.8 copy-start.14
  674.6 33.0 %copy-start.21 = (f32[32,6144]{1,0:T(8,128)}, f32[32,6144]{1,0:T(8,128)S(1)}, u32[]{:S(2)}) copy-start(f32[32,6144]{1,0:T(8,128)S(1)} %fusion.72) | copy-start | bytes 2359300
  674.6 33.0 %collective-permute-start.14 = (f32[32,6144]{1,0:T(8,128)S(1)}, f32[32,6144]{1,0:T(8,128)}, u32[]{:S(2)}, u32[]{:S(2)}) collective-permute-start(f32[32,6144]{1,0:T(8,128)S(1)} %fusion.72), channel_id=1, source_target_pairs={{0,4},{4,8},{8,12},{12,16},{16,20},{20,24},{24,28},{28,0},{1,5},{5... | collective-permute-start | bytes 2359304 | tf_op jit(solution)/shard_map/ppermute | solution.py:20
  674.7 37.3 %collective-permute-start.15 = (f32[32,6144]{1,0:T(8,128)S(1)}, f32[32,6144]{1,0:T(8,128)}, u32[]{:S(2)}, u32[]{:S(2)}) collective-permute-start(f32[32,6144]{1,0:T(8,128)S(1)} %fusion.72), channel_id=1, source_target_pairs={{4,0},{8,4},{12,8},{16,12},{20,16},{24,20},{28,24},{0,28},{5,1},{9... | collective-permute-start | bytes 2359304 | tf_op jit(solution)/shard_map/ppermute | solution.py:22
  750.6 5.9 copy-start.2
  750.6 5.9 copy-start.22
  855.0 23.9 %copy-start.17 = (f32[128,1536]{1,0:T(8,128)}, f32[128,1536]{1,0:T(8,128)S(1)}, u32[]{:S(2)}) copy-start(f32[128,1536]{1,0:T(8,128)S(1)} %fusion.120) | copy-start | bytes 2359300
  870.1 36.1 %collective-permute-start.17 = (f32[32,6144]{1,0:T(8,128)}, f32[32,6144]{1,0:T(8,128)}, u32[]{:S(2)}, u32[]{:S(2)}) collective-permute-start(f32[32,6144]{1,0:T(8,128)} %bitcast.71), channel_id=1, source_target_pairs={{4,0},{8,4},{12,8},{16,12},{20,16},{24,20},{28,24},{0,28},{5,1},{9... | collective-permute-start | bytes 2359304 | tf_op jit(solution)/shard_map/ppermute | solution.py:22
  873.1 34.3 %collective-permute-start.16 = (f32[32,6144]{1,0:T(8,128)}, f32[32,6144]{1,0:T(8,128)}, u32[]{:S(2)}, u32[]{:S(2)}) collective-permute-start(f32[32,6144]{1,0:T(8,128)} %bitcast.71), channel_id=1, source_target_pairs={{0,4},{4,8},{8,12},{12,16},{16,20},{20,24},{24,28},{28,0},{1,5},{5... | collective-permute-start | bytes 2359304 | tf_op jit(solution)/shard_map/ppermute | solution.py:20
  873.1 80.5 %all-to-all-start.4 = ((f32[32,4,1536]{2,0,1:T(8,128)}), f32[32,4,1536]{2,0,1:T(8,128)}, u32[]{:S(2)}, u32[]{:S(2)}) async-start(f32[32,4,1536]{2,0,1:T(8,128)} %get-tuple-element.12), calls=%async_computation.4 | async-start | bytes 1572864 | tf_op jit(solution)/shard_map/all_to_all | solution.py:71
  945.3 11.9 %copy-start.16 = (f32[128,1536]{1,0:T(8,128)S(1)}, f32[128,1536]{1,0:T(8,128)}, u32[]{:S(2)}) copy-start(f32[128,1536]{1,0:T(8,128)} %copy-done.15) | copy-start | bytes 2359300
  950.1 18.6 %copy-start.18 = (f32[128,1536]{1,0:T(8,128)S(1)}, f32[128,1536]{1,0:T(8,128)}, u32[]{:S(2)}) copy-start(f32[128,1536]{1,0:T(8,128)} %copy-done.17) | copy-start | bytes 2359300
  953.6 15.1 %all-to-all-start.5 = ((f32[32,4,1536]{2,0,1:T(8,128)}), f32[32,4,1536]{2,0,1:T(8,128)S(1)}, u32[]{:S(2)}, u32[]{:S(2)}) async-start(f32[32,4,1536]{2,0,1:T(8,128)} %fusion.93), calls=%async_computation.5 | async-start | bytes 1572864 | tf_op jit(solution)/shard_map/all_to_all | solution.py:71
  957.1 134.0 %all-reduce.3.cloned.1.call-start = ((), (), s32[]{:S(2)}) async-start(), calls=%async_computation.8 | async-start | bytes 262144 | tf_op jit(solution)/shard_map/psum | solution.py:86
Sparse Core Ops, SparseCore 0:
  344.4 53.6 all-gather.4
  776.0 53.4 all-gather.6
  970.3 120.7 all-reduce.2
